TPU v7x, 128 devices: a whole 4x4x4 slice. The times are simulated.
128 devices in a mesh: row: 8 (over y, core), col: 16 (over z, x).
Axes of the slice: x: 4, y: 4, z: 4, core: 2. Of those that a mesh axis runs over, the one named last changes fastest.
Arguments:
- ancestor_inverse: float32 [12288, 12288], P('row', 'col')
- factor: bfloat16 [3, 12288, 512], P(None, ('row', 'col')), may hold values from -0.5 to 0.5
- coupling: float32 [3, 512, 512], replicated, may hold values from -0.25 to 0.25
- diagonal_inverse: float32 [3, 512, 512], replicated, may hold values from -6 to 6
- ancestors: int32 [3, 24], replicated, may hold values from -1 to 23, as said below
Outputs:
- block_columns: float32 [3, 12288, 512], P(None, ('row', 'col'))
- block_rows: float32 [3, 12288, 512], P(None, ('col', 'row'))
- node_blocks: float32 [3, 3, 512, 512], replicated
Inputs may be any that keep to these rules, and one draw needn't show every extreme that they name: `ancestors`: row k lists the ancestor block rows of supernode k, blocks of 512 rows: distinct indices in increasing order, then -1 in the slots left. Every block is listed by some supernode.
All inputs are finite; a program needn't handle non-finite values.
Results may differ from a plain program's by a relative error of at most 0.0003.
Values may be sent and summed in bfloat16 or wider, within the bound.
A program may use at most 128 MiB of HBM per device.

v0:
```python
import jax
import jax.numpy as jnp
from jax import lax
from jax.sharding import PartitionSpec as P

highest = lax.Precision.HIGHEST


def broadcast(value, axis, source):
    kept = jnp.where(lax.axis_index(axis) == source, value, 0).astype(value.dtype)
    return lax.psum(kept, axis)


def matmul(left, right):
    return jnp.dot(left, right, precision=highest)


def left_dot(left, right):
    return lax.dot_general(left, right, (((0,), (0,)), ((), ())), precision=highest)


def pair_index(later, earlier):
    return later * (later - 1) // 2 + earlier


def local(ancestor_inverse, factor, coupling, diagonal_inverse, ancestors):
    col_count = lax.axis_size("col")
    row_count = lax.axis_size("row")
    row_index = lax.axis_index("row")
    col_index = lax.axis_index("col")
    nodes_total, piece_rows, sn_width = factor.shape
    rows_here, cols_here = ancestor_inverse.shape
    group_ratio = rows_here // cols_here
    first_row = (row_index * col_count + col_index) * piece_rows
    block_of_row = (first_row + jnp.arange(piece_rows, dtype=jnp.int32)) // sn_width
    source_row = col_index // group_ratio
    block_start = col_index % group_ratio * cols_here
    row_layout = []
    solved = {}
    for current in range(nodes_total):
        listed = jnp.any(ancestors[current][:, None] == block_of_row[None, :], axis=0)
        lower_part = jnp.where(listed[:, None], factor[current], jnp.zeros_like(factor[current]))
        lower_rows = lax.all_gather(lower_part, "col", axis=0, tiled=True)
        own_block = lax.dynamic_slice_in_dim(lower_rows, block_start, cols_here, 0)
        lower_cols = broadcast(own_block, "row", source_row).astype(jnp.float32)
        lower_here = lower_part.astype(jnp.float32)
        product_sum = lax.psum_scatter(
            matmul(ancestor_inverse, lower_cols), "col", scatter_dimension=0, tiled=True
        )
        for earlier in range(current):
            product_sum = product_sum + matmul(
                row_layout[earlier], coupling[pair_index(current, earlier)]
            )
        column = -product_sum
        stacked = jnp.concatenate(row_layout + [column], axis=1)
        summed = lax.psum(left_dot(lower_here, stacked), ("row", "col"))
        crosses = [
            summed[:, earlier * sn_width : (earlier + 1) * sn_width] for earlier in range(current)
        ]
        self_term = summed[:, current * sn_width : (current + 1) * sn_width]
        for earlier in range(current):
            block_value = -crosses[earlier].T
            for inner in range(current):
                block_value = block_value - matmul(
                    solved[earlier, inner], coupling[pair_index(current, inner)]
                )
            solved[earlier, current] = block_value
            solved[current, earlier] = block_value.T
        diag_value = diagonal_inverse[current] - self_term
        for earlier in range(current):
            diag_value = diag_value - left_dot(
                coupling[pair_index(current, earlier)], solved[earlier, current]
            )
        solved[current, current] = diag_value
        row_layout.append(column)
    finished = jnp.stack(row_layout)
    part_rows = piece_rows // row_count
    ratio_cols = col_count // row_count
    split_parts = finished.reshape(nodes_total, row_count, part_rows, sn_width)
    held = lax.all_to_all(split_parts, "row", split_axis=1, concat_axis=1, tiled=True)
    targets = jnp.arange(row_count, dtype=jnp.int32) * ratio_cols + col_index // row_count
    onehot = (targets[:, None] == jnp.arange(col_count, dtype=jnp.int32)[None, :]).astype(
        jnp.float32
    )
    slotted = jnp.einsum("rc,nrqs->ncqs", onehot, held, precision=highest)
    arrived = lax.all_to_all(slotted, "col", split_axis=1, concat_axis=1, tiled=True)
    picked = lax.dynamic_slice_in_dim(arrived, col_index % ratio_cols * row_count, row_count, 1)
    landed = lax.all_to_all(picked, "row", split_axis=1, concat_axis=1, tiled=True)
    mirrored_all = landed.reshape(nodes_total, piece_rows, sn_width)
    node_blocks = jnp.stack(
        [
            jnp.stack([solved[first_node, second_node] for second_node in range(nodes_total)])
            for first_node in range(nodes_total)
        ]
    )
    return (finished, mirrored_all, node_blocks)


def solution(mesh):
    placed = (P("row", "col"), P(None, ("row", "col"), None), P(), P(), P())
    return jax.shard_map(
        local,
        mesh=mesh,
        in_specs=placed,
        out_specs=(P(None, ("row", "col"), None), P(None, ("col", "row"), None), P()),
        check_vma=False,
    )
```

profile of v0, /device:TPU:1, one launch (start us, length us, event | category | flops | bytes accessed | tf_op | source)
XLA Modules:
  0.0 691.0 jit_solution(10552824575240240170)
XLA Ops:
  11.5 45.6 %all-gather.6.cloned.1.call-done = bf16[1536,512]{1,0:T(8,128)(2,1)} async-done(((bf16[96,512]{1,0:T(8,128)(2,1)}), bf16[1536,512]{1,0:T(8,128)(2,1)}) %all-gather.6.cloned.1.call-update) | async-done | bytes 1572880 | tf_op jit(solution)/shard_map/all_gather | solution.py:43
  57.1 2.2 dynamic-slice_select_fusion.1
  59.2 43.3 %all-gather.4.cloned.1.call-done = bf16[1536,512]{1,0:T(8,128)(2,1)} async-done(((bf16[96,512]{1,0:T(8,128)(2,1)}), bf16[1536,512]{1,0:T(8,128)(2,1)}) %all-gather.4.cloned.1.call-update) | async-done | bytes 1572880 | tf_op jit(solution)/shard_map/all_gather | solution.py:43
  102.5 2.1 dynamic-slice_select_fusion.2
  104.7 43.3 %all-gather.8.cloned.1.call-done = bf16[1536,512]{1,0:T(8,128)(2,1)} async-done(((bf16[96,512]{1,0:T(8,128)(2,1)}), bf16[1536,512]{1,0:T(8,128)(2,1)}) %all-gather.8.cloned.1.call-update) | async-done | bytes 1572880 | tf_op jit(solution)/shard_map/all_gather | solution.py:43
  148.0 2.1 dynamic-slice_select_fusion
  150.3 66.0 %all-reduce.7.cloned.1.call-done = (bf16[768,512]{1,0:T(8,128)(2,1)}, bf16[768,512]{1,0:T(8,128)(2,1)}, bf16[768,512]{1,0:T(8,128)(2,1)}) async-done(((bf16[768,512]{1,0:T(8,128)(2,1)}, bf16[768,512]{1,0:T(8,128)(2,1)}, bf16[768,512]{1,0:T(8,128)(2,1)}), (bf16[768,512]{1,0:T(8,128)(2,1)}, bf16[768,512]{1,0:T(8,128)(2,1)}, bf16[768,512]{1,0:T(8,128)(2,1)})) %all-reduce.7.cloned.1.call-update) | async-done | bytes 2359312 | tf_op jit(solution)/shard_map/psum | solution.py:11
  216.2 6.7 convolution_bitcast_fusion.2
  222.9 2.3 copy.104
  225.3 6.7 convolution_bitcast_fusion.1
  232.0 2.4 copy.106
  234.5 6.7 convolution_bitcast_fusion
  241.2 2.4 copy.108
  244.1 57.1 %reduce-scatter.10.cloned.1.call-done = f32[96,512]{1,0:T(8,128)} async-done(((f32[1536,512]{1,0:T(8,128)}), f32[96,512]{1,0:T(8,128)}) %reduce-scatter.10.cloned.1.call-update) | async-done | bytes 196624 | tf_op jit(solution)/shard_map/reduce_scatter | solution.py:47
  301.2 78.3 %reduce-scatter.12.cloned.1.call-done = f32[96,512]{1,0:T(8,128)} async-done(((f32[1536,512]{1,0:T(8,128)}), f32[96,512]{1,0:T(8,128)}) %reduce-scatter.12.cloned.1.call-update) | async-done | bytes 196624 | tf_op jit(solution)/shard_map/reduce_scatter | solution.py:47
  381.3 77.3 %reduce-scatter.14.cloned.1.call-done = f32[96,512]{1,0:T(8,128)} async-done(((f32[1536,512]{1,0:T(8,128)}), f32[96,512]{1,0:T(8,128)}) %reduce-scatter.14.cloned.1.call-update) | async-done | bytes 196624 | tf_op jit(solution)/shard_map/reduce_scatter | solution.py:47
  458.6 1.8 convolution_add_fusion.1
  461.9 2.3 fusion.45
  464.2 3.1 fusion.38
  475.2 6.7 all-to-all-start
  481.9 15.6 %all-to-all-done = f32[3,8,12,512]{3,2,0,1:T(8,128)} async-done(((f32[3,8,12,512]{3,2,0,1:T(8,128)}), f32[3,8,12,512]{3,2,0,1:T(8,128)}, u32[]{:S(2)}, u32[]{:S(2)}) %all-to-all-start) | async-done | bytes 589856 | tf_op jit(solution)/shard_map/all_to_all | solution.py:80
  497.5 2.1 convolution_bitcast_fusion.3
  499.6 1.9 copy.80
  501.5 4.8 all-to-all-start.1
  506.3 21.0 %all-to-all-done.1 = f32[3,16,12,512]{3,2,0,1:T(8,128)} async-done(((f32[3,16,12,512]{3,2,0,1:T(8,128)}), f32[3,16,12,512]{3,2,0,1:T(8,128)}, u32[]{:S(2)}, u32[]{:S(2)}) %all-to-all-start.1) | async-done | bytes 1179680 | tf_op jit(solution)/shard_map/all_to_all | solution.py:86
  527.3 2.1 constant_dynamic-slice_fusion
  529.4 9.0 %all-to-all-start.2 = ((f32[3,8,12,512]{3,2,0,1:T(8,128)}), f32[3,8,12,512]{3,2,0,1:T(8,128)}, u32[]{:S(2)}, u32[]{:S(2)}) async-start(f32[3,8,12,512]{3,2,0,1:T(8,128)} %constant_dynamic-slice_fusion), calls=%async_computation.2 | async-start | bytes 1572864 | tf_op jit(solution)/shard_map/all_to_all | solution.py:88
  538.4 2.4 slice.71
  540.8 2.6 copy.110
  543.4 1.8 pad_maximum_fusion.2
  545.1 5.7 all-to-all-done.2
  550.9 2.2 copy.81
  553.0 2.0 reshape.46
  555.1 83.9 %all-reduce.5.cloned.1.call-done = (f32[512,1536]{1,0:T(8,128)}, f32[512,512]{1,0:T(8,128)}, f32[512,1024]{0,1:T(8,128)}) async-done(((f32[512,1536]{1,0:T(8,128)}, f32[512,512]{1,0:T(8,128)}, f32[512,1024]{0,1:T(8,128)}), (f32[512,1536]{1,0:T(8,128)}, f32[512,512]{1,0:T(8,128)}, f32[512,1024]{0,1:T(8,128)})) %all-reduce.5.cloned.1.call-update) | async-done | bytes 6291472 | tf_op jit(solution)/shard_map/psum | solution.py:56
  638.9 3.8 bitcast_subtract_fusion.7
  642.7 1.9 fusion.14
  644.6 1.9 fusion.18
  646.6 1.9 fusion.20
  648.5 2.0 fusion.3
  651.5 2.1 fusion.12
  653.7 3.1 fusion.2
  656.8 2.3 fusion.7
  659.1 2.3 fusion.60
  661.4 2.6 copy.85
  663.9 3.8 maximum_bitcast_fusion.1
  667.8 3.6 copy.95
  671.3 4.3 fusion.1
  679.1 4.9 pad_maximum_fusion
  (78 shorter events, 20.5 us)
Async XLA Ops:
  7.2 49.9 %all-gather.6.cloned.1.call-start = ((), (), s32[]{:S(2)}) async-start(), calls=%async_computation.7 | async-start | bytes 1671168 | tf_op jit(solution)/shard_map/all_gather | solution.py:43
  9.9 92.6 %all-gather.4.cloned.1.call-start = ((), (), s32[]{:S(2)}) async-start(), calls=%async_computation.6 | async-start | bytes 1671168 | tf_op jit(solution)/shard_map/all_gather | solution.py:43
  10.7 137.4 %all-gather.8.cloned.1.call-start = ((), (), s32[]{:S(2)}) async-start(), calls=%async_computation.8 | async-start | bytes 1671168 | tf_op jit(solution)/shard_map/all_gather | solution.py:43
  11.4 204.8 %all-reduce.7.cloned.1.call-start = ((), (), s32[]{:S(2)}) async-start(), calls=%async_computation.13 | async-start | bytes 4718592 | tf_op jit(solution)/shard_map/psum | solution.py:11
  150.2 151.0 %reduce-scatter.10.cloned.1.call-start = ((), (), s32[]{:S(2)}) async-start(), calls=%async_computation.9 | async-start | bytes 3342336 | tf_op jit(solution)/shard_map/reduce_scatter | solution.py:47
  225.3 154.3 %reduce-scatter.12.cloned.1.call-start = ((), (), s32[]{:S(2)}) async-start(), calls=%async_computation.10 | async-start | bytes 3342336 | tf_op jit(solution)/shard_map/reduce_scatter | solution.py:47
  234.4 224.1 %reduce-scatter.14.cloned.1.call-start = ((), (), s32[]{:S(2)}) async-start(), calls=%async_computation.11 | async-start | bytes 3342336 | tf_op jit(solution)/shard_map/reduce_scatter | solution.py:47
  243.6 136.0 %copy-start = (f32[3,512,512]{2,1,0:T(8,128)S(1)}, f32[3,512,512]{2,1,0:T(8,128)}, u32[]{:S(2)}) copy-start(f32[3,512,512]{2,1,0:T(8,128)} %param.7) | copy-start | bytes 9437188
  243.6 395.3 %all-reduce.5.cloned.1.call-start = ((), (), s32[]{:S(2)}) async-start(), calls=%async_computation.12 | async-start | bytes 12582912 | tf_op jit(solution)/shard_map/psum | solution.py:56
  301.2 159.9 %copy-start.16 = (f32[96,512]{1,0:T(8,128)S(1)}, f32[96,512]{1,0:T(8,128)}, u32[]{:S(2)}) copy-start(f32[96,512]{1,0:T(8,128)} %reduce-scatter.10.cloned.1.call-done) | copy-start | bytes 589828
  458.6 3.3 copy-start.20
  458.6 5.7 copy-start.22
  461.1 6.2 copy-start.17
  461.9 5.5 copy-start.19
  461.9 5.5 copy-start.21
  469.0 0.9 copy-start.18
  475.2 22.3 %all-to-all-start = ((f32[3,8,12,512]{3,2,0,1:T(8,128)}), f32[3,8,12,512]{3,2,0,1:T(8,128)}, u32[]{:S(2)}, u32[]{:S(2)}) async-start(f32[3,8,12,512]{3,2,0,1:T(8,128)} %copy.78), calls=%async_computation | async-start | bytes 1572864 | tf_op jit(solution)/shard_map/all_to_all | solution.py:80
  501.5 25.8 %all-to-all-start.1 = ((f32[3,16,12,512]{3,2,0,1:T(8,128)}), f32[3,16,12,512]{3,2,0,1:T(8,128)}, u32[]{:S(2)}, u32[]{:S(2)}) async-start(f32[3,16,12,512]{3,2,0,1:T(8,128)} %copy.80), calls=%async_computation.1 | async-start | bytes 3145728 | tf_op jit(solution)/shard_map/all_to_all | solution.py:86
  529.4 21.4 %all-to-all-start.2 = ((f32[3,8,12,512]{3,2,0,1:T(8,128)}), f32[3,8,12,512]{3,2,0,1:T(8,128)}, u32[]{:S(2)}, u32[]{:S(2)}) async-start(f32[3,8,12,512]{3,2,0,1:T(8,128)} %constant_dynamic-slice_fusion), calls=%async_computation.2 | async-start | bytes 1572864 | tf_op jit(solution)/shard_map/all_to_all | solution.py:88
  642.7 5.8 copy-start.1
  642.7 3.8 copy-start.8
  642.7 3.8 copy-start.9
  644.6 3.9 copy-start.10
  644.6 3.9 copy-start.11
  646.6 12.5 %copy-start.3 = (f32[512,512]{0,1:T(8,128)}, f32[512,512]{0,1:T(8,128)S(1)}, u32[]{:S(2)}) copy-start(f32[512,512]{0,1:T(8,128)S(1)} %fusion.18) | copy-start | bytes 3145732
  648.5 5.1 copy-start.6
  650.5 1.0 copy-start.7
  653.7 5.4 copy-start.4
  671.3 4.3 copy-start.2
  671.3 4.3 copy-start.12
  671.3 4.3 copy-start.15
  675.7 1.2 copy-start.13
  675.7 1.5 copy-start.14
  677.2 1.9 copy-start.5
Sparse Core Ops, SparseCore 0:
  10.7 46.3 all-gather.5
  59.2 43.3 all-gather.3
  104.7 43.3 all-gather.7
  151.0 65.1 all-reduce.6
  225.4 75.7 reduce-scatter.9
  304.4 75.1 reduce-scatter.11
  383.4 75.0 reduce-scatter.13
  469.1 169.7 all-reduce.4
where the time goes:
time: 699 us; the launch traced here: 691 us
  waiting for transfers between devices  539 us (77%)
  matrix products  54.5 us (8%)
  local copies, waits for them, and re-layouts  36 us (5%)
  other arithmetic  26 us (4%)
  starting transfers between devices  21.2 us (3%)
  between operations  14.7 us (2%)
    reduce_scatter x3, waiting for transfers between devices, local(): lax.psum_scatter(matmul(ancestor_inverse, lower_cols), 'col', scatter_dim...  213 us
    all_gather x3, waiting for transfers between devices, local(): lower_rows = lax.all_gather(lower_part, 'col', axis=0, tiled=True)  132 us
    psum x1, waiting for transfers between devices, local(): summed = lax.psum(left_dot(lower_here, stacked), ('row', 'col'))  83.9 us
    psum x1, waiting for transfers between devices, broadcast(): return lax.psum(kept, axis)  66 us
    dot_general x11, matrix products, matmul(): return jnp.dot(left, right, precision=highest)  36 us
    all_to_all x1, waiting for transfers between devices, local(): lax.all_to_all(slotted, 'col', split_axis=1, concat_axis=1, tiled=True)  21 us
    dot_general x6, matrix products, left_dot(): lax.dot_general(left, right, (((0,), (0,)), ((), ())), precision=highest)  16.5 us
    all_to_all x1, waiting for transfers between devices, local(): lax.all_to_all(split_parts, 'row', split_axis=1, concat_axis=1, tiled=True)  15.6 us
  transfers between devices with their start and end apart: 11, of which 11 were waited for; matrix products, arithmetic and copies ran while one was open for 7% of the time, Pallas kernels for 0%

commit v1 on v0

--- a/solution.py
+++ b/solution.py
@@ -83,7 +83,10 @@
         jnp.float32
     )
     slotted = jnp.einsum("rc,nrqs->ncqs", onehot, held, precision=highest)
-    arrived = lax.all_to_all(slotted, "col", split_axis=1, concat_axis=1, tiled=True)
+    arrived = jnp.concatenate(
+        lax.all_to_all(jnp.stack(jnp.split(slotted, lax.axis_size("col"), axis=1)), "col", 0, 0),
+        axis=1,
+    )
     picked = lax.dynamic_slice_in_dim(arrived, col_index % ratio_cols * row_count, row_count, 1)
     landed = lax.all_to_all(picked, "row", split_axis=1, concat_axis=1, tiled=True)
     mirrored_all = landed.reshape(nodes_total, piece_rows, sn_width)

time: 699 us -> 707 us (1.011)
  local copies, waits for them, and re-layouts: 36 us -> 45.5 us
    psum x1, waiting for transfers between devices: 83.9 us -> 98.9 us  [local(): summed = lax.psum(left_dot(lower_here, stacked), ('row', 'col'))]
    all_to_all x1, waiting for transfers between devices: 15.6 us -> 5.74 us  [local(): lax.all_to_all(split_parts, 'row', split_axis=1, concat_axis=1, tiled=True)]
    unnamed x50 -> x55, local copies, waits for them, and re-layouts: 14.4 us -> 23.9 us
    reduce_scatter x3, waiting for transfers between devices: 213 us -> 205 us  [local(): lax.psum_scatter(matmul(ancestor_inverse, lower_cols), 'col', scatter_dim...]
  transfers between devices with their start and end apart: 11 -> 11, of which waited for: 11 -> 11; matrix products, arithmetic and copies ran while one was open for 7% -> 9% of each run, Pallas kernels for 0% -> 0%
where the time goes in v1:
time: 707 us; the launch traced here: 700 us
  waiting for transfers between devices  537 us (76%)
  matrix products  58.1 us (8%)
  local copies, waits for them, and re-layouts  45.5 us (6%)
  other arithmetic  27 us (4%)
  starting transfers between devices  18.3 us (3%)
  between operations  14.7 us (2%)
    reduce_scatter x3, waiting for transfers between devices, local(): lax.psum_scatter(matmul(ancestor_inverse, lower_cols), 'col', scatter_dim...  205 us
    all_gather x3, waiting for transfers between devices, local(): lower_rows = lax.all_gather(lower_part, 'col', axis=0, tiled=True)  132 us
    psum x1, waiting for transfers between devices, local(): summed = lax.psum(left_dot(lower_here, stacked), ('row', 'col'))  98.9 us
    psum x1, waiting for transfers between devices, broadcast(): return lax.psum(kept, axis)  66 us
    dot_general x11, matrix products, matmul(): return jnp.dot(left, right, precision=highest)  36.6 us
    unnamed x55, local copies, waits for them, and re-layouts  23.9 us
    all_to_all x1, waiting for transfers between devices, local(): lax.all_to_all(jnp.stack(jnp.split(slotted, lax.axis_size('col'), axis=1)...  20.8 us
    dot_general x6, matrix products, left_dot(): lax.dot_general(left, right, (((0,), (0,)), ((), ())), precision=highest)  19.4 us
  transfers between devices with their start and end apart: 11, of which 11 were waited for; matrix products, arithmetic and copies ran while one was open for 9% of the time, Pallas kernels for 0%

profile of v1, /device:TPU:1, one launch (start us, length us, event | category | flops | bytes accessed | tf_op | source)
XLA Modules:
  0.0 700.5 jit_solution(2018891398065626859)
XLA Ops:
  8.1 1.8 bitcast_select_fusion.1
  11.5 45.6 %all-gather.6.cloned.1.call-done = bf16[1536,512]{1,0:T(8,128)(2,1)} async-done(((bf16[96,512]{1,0:T(8,128)(2,1)}), bf16[1536,512]{1,0:T(8,128)(2,1)}) %all-gather.6.cloned.1.call-update) | async-done | bytes 1572880 | tf_op jit(solution)/shard_map/all_gather | solution.py:43
  57.1 2.2 dynamic-slice_select_fusion.1
  59.3 43.3 %all-gather.4.cloned.1.call-done = bf16[1536,512]{1,0:T(8,128)(2,1)} async-done(((bf16[96,512]{1,0:T(8,128)(2,1)}), bf16[1536,512]{1,0:T(8,128)(2,1)}) %all-gather.4.cloned.1.call-update) | async-done | bytes 1572880 | tf_op jit(solution)/shard_map/all_gather | solution.py:43
  102.5 2.1 dynamic-slice_select_fusion.2
  104.7 43.4 %all-gather.8.cloned.1.call-done = bf16[1536,512]{1,0:T(8,128)(2,1)} async-done(((bf16[96,512]{1,0:T(8,128)(2,1)}), bf16[1536,512]{1,0:T(8,128)(2,1)}) %all-gather.8.cloned.1.call-update) | async-done | bytes 1572880 | tf_op jit(solution)/shard_map/all_gather | solution.py:43
  148.0 2.1 dynamic-slice_select_fusion
  150.3 66.0 %all-reduce.7.cloned.1.call-done = (bf16[768,512]{1,0:T(8,128)(2,1)}, bf16[768,512]{1,0:T(8,128)(2,1)}, bf16[768,512]{1,0:T(8,128)(2,1)}) async-done(((bf16[768,512]{1,0:T(8,128)(2,1)}, bf16[768,512]{1,0:T(8,128)(2,1)}, bf16[768,512]{1,0:T(8,128)(2,1)}), (bf16[768,512]{1,0:T(8,128)(2,1)}, bf16[768,512]{1,0:T(8,128)(2,1)}, bf16[768,512]{1,0:T(8,128)(2,1)})) %all-reduce.7.cloned.1.call-update) | async-done | bytes 2359312 | tf_op jit(solution)/shard_map/psum | solution.py:11
  216.2 6.7 convolution_bitcast_fusion.2
  222.9 2.3 copy.108
  225.3 6.7 convolution_bitcast_fusion.1
  232.0 2.4 copy.110
  234.9 6.8 convolution_bitcast_fusion
  241.8 2.4 copy.112
  244.2 57.0 %reduce-scatter.10.cloned.1.call-done = f32[96,512]{1,0:T(8,128)} async-done(((f32[1536,512]{1,0:T(8,128)}), f32[96,512]{1,0:T(8,128)}) %reduce-scatter.10.cloned.1.call-update) | async-done | bytes 196624 | tf_op jit(solution)/shard_map/reduce_scatter | solution.py:47
  301.2 78.3 %reduce-scatter.12.cloned.1.call-done = f32[96,512]{1,0:T(8,128)} async-done(((f32[1536,512]{1,0:T(8,128)}), f32[96,512]{1,0:T(8,128)}) %reduce-scatter.12.cloned.1.call-update) | async-done | bytes 196624 | tf_op jit(solution)/shard_map/reduce_scatter | solution.py:47
  379.6 1.8 fusion.5
  385.4 3.4 fusion.45
  388.8 69.8 %reduce-scatter.14.cloned.1.call-done = f32[96,512]{1,0:T(8,128)} async-done(((f32[1536,512]{1,0:T(8,128)}), f32[96,512]{1,0:T(8,128)}) %reduce-scatter.14.cloned.1.call-update) | async-done | bytes 196624 | tf_op jit(solution)/shard_map/reduce_scatter | solution.py:47
  465.5 6.7 all-to-all-start
  472.2 2.5 fusion.70
  474.7 4.2 fusion.38
  478.9 5.7 all-to-all-done
  484.6 2.1 convolution_bitcast_fusion.3
  497.8 4.6 all-to-all-start.1
  502.4 20.8 %all-to-all-done.1 = f32[16,3,1,12,512]{4,2,3,1,0:T(1,128)} async-done(((f32[16,3,1,12,512]{4,2,3,1,0:T(1,128)}), f32[16,3,1,12,512]{4,2,3,1,0:T(1,128)}, u32[]{:S(2)}, u32[]{:S(2)}) %all-to-all-start.1) | async-done | bytes 1179680 | tf_op jit(solution)/shard_map/all_to_all | solution.py:87
  525.6 6.3 all-to-all-start.2
  531.9 2.4 slice.71
  534.3 2.6 copy.114
  536.9 1.8 pad_maximum_fusion.2
  538.7 6.6 all-to-all-done.2
  545.3 2.2 copy.84
  547.5 2.0 reshape.49
  549.5 98.9 %all-reduce.5.cloned.1.call-done = (f32[512,1536]{1,0:T(8,128)}, f32[512,512]{1,0:T(8,128)}, f32[512,1024]{0,1:T(8,128)}) async-done(((f32[512,1536]{1,0:T(8,128)}, f32[512,512]{1,0:T(8,128)}, f32[512,1024]{0,1:T(8,128)}), (f32[512,1536]{1,0:T(8,128)}, f32[512,512]{1,0:T(8,128)}, f32[512,1024]{0,1:T(8,128)})) %all-reduce.5.cloned.1.call-update) | async-done | bytes 6291472 | tf_op jit(solution)/shard_map/psum | solution.py:56
  648.4 3.8 bitcast_subtract_fusion.7
  652.2 1.9 fusion.14
  654.1 1.9 fusion.18
  656.1 1.9 fusion.20
  658.0 2.0 fusion.3
  661.0 2.1 fusion.12
  663.1 3.1 fusion.2
  666.2 2.3 fusion.7
  668.5 2.3 fusion.76
  670.8 2.5 copy.88
  673.4 3.8 maximum_bitcast_fusion.1
  677.2 3.6 copy.98
  680.8 4.3 fusion.1
  688.5 4.9 pad_maximum_fusion
  (84 shorter events, 32.1 us)
Async XLA Ops:
  7.2 49.9 %all-gather.6.cloned.1.call-start = ((), (), s32[]{:S(2)}) async-start(), calls=%async_computation.7 | async-start | bytes 1671168 | tf_op jit(solution)/shard_map/all_gather | solution.py:43
  9.9 92.6 %all-gather.4.cloned.1.call-start = ((), (), s32[]{:S(2)}) async-start(), calls=%async_computation.6 | async-start | bytes 1671168 | tf_op jit(solution)/shard_map/all_gather | solution.py:43
  10.7 137.4 %all-gather.8.cloned.1.call-start = ((), (), s32[]{:S(2)}) async-start(), calls=%async_computation.8 | async-start | bytes 1671168 | tf_op jit(solution)/shard_map/all_gather | solution.py:43
  11.4 204.8 %all-reduce.7.cloned.1.call-start = ((), (), s32[]{:S(2)}) async-start(), calls=%async_computation.13 | async-start | bytes 4718592 | tf_op jit(solution)/shard_map/psum | solution.py:11
  150.2 151.0 %reduce-scatter.10.cloned.1.call-start = ((), (), s32[]{:S(2)}) async-start(), calls=%async_computation.9 | async-start | bytes 3342336 | tf_op jit(solution)/shard_map/reduce_scatter | solution.py:47
  225.3 154.3 %reduce-scatter.12.cloned.1.call-start = ((), (), s32[]{:S(2)}) async-start(), calls=%async_computation.10 | async-start | bytes 3342336 | tf_op jit(solution)/shard_map/reduce_scatter | solution.py:47
  234.4 224.2 %reduce-scatter.14.cloned.1.call-start = ((), (), s32[]{:S(2)}) async-start(), calls=%async_computation.11 | async-start | bytes 3342336 | tf_op jit(solution)/shard_map/reduce_scatter | solution.py:47
  244.1 135.4 %copy-start = (f32[3,512,512]{2,1,0:T(8,128)S(1)}, f32[3,512,512]{2,1,0:T(8,128)}, u32[]{:S(2)}) copy-start(f32[3,512,512]{2,1,0:T(8,128)} %param.7) | copy-start | bytes 9437188
  301.2 157.4 %copy-start.16 = (f32[96,512]{1,0:T(8,128)S(1)}, f32[96,512]{1,0:T(8,128)}, u32[]{:S(2)}) copy-start(f32[96,512]{1,0:T(8,128)} %reduce-scatter.10.cloned.1.call-done) | copy-start | bytes 589828
  465.5 19.1 %all-to-all-start = ((f32[3,8,12,512]{3,2,0,1:T(8,128)}), f32[3,8,12,512]{3,2,0,1:T(8,128)}, u32[]{:S(2)}, u32[]{:S(2)}) async-start(f32[3,8,12,512]{3,2,0,1:T(8,128)} %copy.80), calls=%async_computation | async-start | bytes 1572864 | tf_op jit(solution)/shard_map/all_to_all | solution.py:80
  472.2 176.2 %all-reduce.5.cloned.1.call-start = ((), (), s32[]{:S(2)}) async-start(), calls=%async_computation.12 | async-start | bytes 12582912 | tf_op jit(solution)/shard_map/psum | solution.py:56
  497.8 25.3 %all-to-all-start.1 = ((f32[16,3,1,12,512]{4,2,3,1,0:T(1,128)}), f32[16,3,1,12,512]{4,2,3,1,0:T(1,128)}, u32[]{:S(2)}, u32[]{:S(2)}) async-start(f32[16,3,1,12,512]{4,2,3,1,0:T(1,128)} %fusion.49), calls=%async_computation.1 | async-start | bytes 2359296 | tf_op jit(solution)/shard_map/all_to_all | solution.py:87
  525.6 11.3 %copy-start.17 = (f32[96,512]{1,0:T(8,128)S(1)}, f32[96,512]{1,0:T(8,128)}, u32[]{:S(2)}) copy-start(f32[96,512]{1,0:T(8,128)} %fusion.4) | copy-start | bytes 589828
  525.6 19.7 %all-to-all-start.2 = ((f32[3,8,12,512]{3,2,0,1:T(8,128)}), f32[3,8,12,512]{3,2,0,1:T(8,128)}, u32[]{:S(2)}, u32[]{:S(2)}) async-start(f32[3,8,12,512]{3,2,0,1:T(8,128)} %bitcast.230), calls=%async_computation.2 | async-start | bytes 1572864 | tf_op jit(solution)/shard_map/all_to_all | solution.py:91
  652.2 5.8 copy-start.1
  652.2 3.8 copy-start.8
  652.2 3.8 copy-start.9
  654.1 3.9 copy-start.10
  654.1 3.9 copy-start.11
  656.0 12.5 %copy-start.3 = (f32[512,512]{0,1:T(8,128)}, f32[512,512]{0,1:T(8,128)S(1)}, u32[]{:S(2)}) copy-start(f32[512,512]{0,1:T(8,128)S(1)} %fusion.18) | copy-start | bytes 3145732
  658.0 5.1 copy-start.6
  660.0 1.0 copy-start.7
  663.1 5.4 copy-start.4
  680.8 4.3 copy-start.2
  680.8 4.3 copy-start.12
  680.8 4.3 copy-start.15
  685.1 1.2 copy-start.13
  685.1 1.5 copy-start.14
  686.7 1.9 copy-start.5
Sparse Core Ops, SparseCore 0:
  10.7 46.3 all-gather.5
  59.2 43.3 all-gather.3
  104.7 43.3 all-gather.7
  151.0 65.1 all-reduce.6
  225.4 75.7 reduce-scatter.9
  304.4 75.1 reduce-scatter.11
  383.4 75.0 reduce-scatter.13
  479.0 169.3 all-reduce.4
